TPU v7x, 128 devices: a whole 4x4x4 slice. The times are simulated.
128 devices in a mesh: row: 16 (over z_hi, y, core), col: 8 (over z_lo, x).
Axes of the slice: x: 4, y: 4, z: 4 (z_hi: 2, z_lo: 2; z = z_hi * 2 + z_lo), core: 2. Of those that a mesh axis runs over, the one named last changes fastest.
Arguments:
- multispectral: bfloat16 [2, 32768, 4096], P(None, 'row', 'col'), may hold values from -6 to 6
- hyperspectral: bfloat16 [96, 8192, 1024], P(None, 'row', 'col'), may hold values from -6 to 6
- row_start: float32 [32768, 128], P(('row', 'col')), may hold values from -6 to 6
- col_factor: bfloat16 [4096, 128], P('col', 'row'), may hold values from -0.09375 to 0.09375
- band_factor: float32 [96, 128], replicated, may hold values from -2 to 2
- response: float32 [2, 96], replicated, may hold values from 0.2 to 1
- blur_taps: float32 [9], replicated, may hold values from 0.2 to 1
- offsets: int32 [9], replicated, may hold values from -8 to 8, as said below
Outputs:
- row_factor: float32 [32768, 128], P(('row', 'col'))
- residual: float32 [32768, 128], P(('row', 'col'))
Inputs may be any that keep to these rules, and one draw needn't show every extreme that they name: 9 distinct offsets; -8 and 8 are always among them.
All inputs are finite; a program needn't handle non-finite values.
Results may differ from a plain program's by a relative error of at most 0.0023.
Values may be sent and summed in bfloat16 or wider, within the bound.
A program may use at most 128 MiB of HBM per device.

v0:
```python
import jax
import jax.numpy as jnp
from jax import lax
from jax.sharding import PartitionSpec as P

DEC = 4
W = 8
ITERS = 4
RIDGE_TERM = 0.1
FULL_PRECISION = lax.Precision.HIGHEST


def extended(cells, sides, width):
    for axis, dim in sides:
        count = lax.axis_size(axis)
        head = lax.slice_in_dim(cells, 0, width, axis=dim)
        tail = lax.slice_in_dim(cells, cells.shape[dim] - width, cells.shape[dim], axis=dim)
        cells = jnp.concatenate(
            [
                lax.ppermute(tail, axis, [(i, (i + 1) % count) for i in range(count)]),
                cells,
                lax.ppermute(head, axis, [((i + 1) % count, i) for i in range(count)]),
            ],
            axis=dim,
        )
    return cells


def down_matrix(weights, offsets, rows_out, rows_in):
    outer = lax.broadcasted_iota(jnp.int32, (rows_out, rows_in), 0)
    inner = lax.broadcasted_iota(jnp.int32, (rows_out, rows_in), 1)
    total = jnp.zeros((rows_out, rows_in), jnp.float32)
    for number in range(weights.shape[0]):
        target = DEC * outer + offsets[number] + W
        total = total + jnp.where(inner == target, weights[number], jnp.float32(0.0))
    return total


def up_matrix(weights, offsets, rows_in, low_margin):
    rows_out = (rows_in - 2 * low_margin) * DEC
    outer = lax.broadcasted_iota(jnp.int32, (rows_out, rows_in), 0)
    inner = lax.broadcasted_iota(jnp.int32, (rows_out, rows_in), 1)
    total = jnp.zeros((rows_out, rows_in), jnp.float32)
    for number in range(weights.shape[0]):
        target = outer + DEC * low_margin - offsets[number]
        total = total + jnp.where(DEC * inner == target, weights[number], jnp.float32(0.0))
    return total


def apply_band(matrix, values):
    return jnp.dot(matrix, values.astype(jnp.float32), precision=FULL_PRECISION)


def body(
    multispectral, hyperspectral, row_start, col_factor, band_factor, response, blur_taps, offsets
):
    low_reach = (W + DEC - 1) // DEC
    columns = lax.all_gather(col_factor, "row", axis=1, tiled=True)
    column_wide = extended(columns, (("col", 0),), W)
    column_down = down_matrix(blur_taps, offsets, columns.shape[0] // DEC, column_wide.shape[0])
    coarse_columns = apply_band(column_down, column_wide)
    merged = jnp.dot(response, band_factor, precision=FULL_PRECISION)
    multi_pairs = (merged[:, None, :] * columns.astype(jnp.float32)[None, :, :]).astype(
        jnp.bfloat16
    )
    hyper_pairs = (band_factor[:, None, :] * coarse_columns[None, :, :]).astype(jnp.bfloat16)
    multi_part = jnp.einsum(
        "kij,kjr->ir", multispectral, multi_pairs, preferred_element_type=jnp.float32
    )
    hyper_part = jnp.einsum(
        "kij,kjr->ir", hyperspectral, hyper_pairs, preferred_element_type=jnp.float32
    )
    column_part = jnp.einsum("jr,js->rs", columns, columns, preferred_element_type=jnp.float32)
    coarse_part = jnp.einsum("jr,js->rs", coarse_columns, coarse_columns, precision=FULL_PRECISION)
    column_gram, coarse_gram = lax.psum((column_part, coarse_part), "col")
    band_gram = jnp.dot(band_factor.T, band_factor, precision=FULL_PRECISION)
    merged_gram = jnp.dot(merged.T, merged, precision=FULL_PRECISION)
    hyper_gram = coarse_gram * band_gram
    multi_gram = column_gram * merged_gram
    multi_sums, hyper_sums = lax.psum((multi_part, hyper_part), "col")
    start_rows = lax.all_gather(row_start, "col", axis=0, tiled=True)

    def fine_rim(values, breadth):
        return extended(values, (("row", 0),), breadth)

    def coarse_rim(values):
        return extended(values, (("row", 0),), low_reach)

    def inner_sum(first_field, second_field):
        return lax.psum(jnp.sum(first_field * second_field), "row")

    fine_rows = start_rows.shape[0]
    coarse_rows = fine_rows // DEC
    lifting = up_matrix(blur_taps, offsets, coarse_rows + 2 * low_reach, low_reach)
    lowering = down_matrix(blur_taps, offsets, coarse_rows, fine_rows + 2 * W)

    def operate(values):
        fine_wide = fine_rim(values, W)
        coarse_wide = coarse_rim(apply_band(lowering, fine_wide))
        restored = apply_band(lifting, coarse_wide)
        return (
            jnp.dot(restored, hyper_gram, precision=FULL_PRECISION)
            + jnp.dot(values, multi_gram, precision=FULL_PRECISION)
            + RIDGE_TERM * values
        )

    right_side = apply_band(lifting, coarse_rim(hyper_sums)) + multi_sums
    solution = start_rows
    residual = right_side - operate(solution)
    direction = residual
    norm_now = inner_sum(residual, residual)
    for iteration in range(ITERS):
        mapped = operate(direction)
        step_size = norm_now / inner_sum(direction, mapped)
        solution = solution + step_size * direction
        residual = residual - step_size * mapped
        norm_next = inner_sum(residual, residual)
        direction = residual + norm_next / norm_now * direction
        norm_now = norm_next
    portion = solution.shape[0] // lax.axis_size("col")
    corner = lax.axis_index("col") * portion
    solution = lax.dynamic_slice_in_dim(solution, corner, portion, 0)
    residual = lax.dynamic_slice_in_dim(residual, corner, portion, 0)
    return (solution, residual)


def solution(mesh):
    in_specs = (
        P(None, "row", "col"),
        P(None, "row", "col"),
        P(("row", "col"), None),
        P("col", "row"),
        P(),
        P(),
        P(),
        P(),
    )
    out_specs = (P(("row", "col"), None), P(("row", "col"), None))
    return jax.shard_map(body, mesh=mesh, in_specs=in_specs, out_specs=out_specs, check_vma=False)
```

profile of v0, /device:TPU:0, one launch (start us, length us, event | category | flops | bytes accessed | tf_op | source)
XLA Modules:
  0.0 721.7 jit_solution(4614198952941534308)
XLA Ops:
  7.2 25.9 %all_gather.7 = bf16[512,128]{0,1:T(8,128)(2,1)S(1)} all-gather(bf16[512,8]{0,1:T(8,128)(2,1)} %param.11), channel_id=1, replica_groups=mesh['row'=16,'col'=8] {'row'}, dimensions={1}, use_global_device_ids=true | all-gather | bytes 139264 | tf_op jit(solution)/shard_map/all_gather | solution.py:58
  52.6 6.3 fusion.50
  59.9 8.2 %fusion.14 = f32[512,128]{0,1:T(8,128)} fusion(bf16[96,512,128]{2,1,0:T(8,128)(2,1)} %param.9, f32[128,128]{0,1:T(8,128)S(1)} %copy.10, f32[96,128]{1,0:T(8,128)S(1)} %copy-done.4), kind=kOutput, calls=%fused_computation.33 | convolution fusion | flops 1613758464 | bytes 12959744 | tf_op jit(solution)/shard_map/kij,kjr->ir/dot_general | solution.py:70
  79.9 62.0 %all-reduce.4.cloned.1.call-done = (f32[128,128]{1,0:T(8,128)}, f32[128,128]{1,0:T(8,128)}, f32[2048,128]{1,0:T(8,128)}, f32[512,128]{0,1:T(8,128)}) async-done(((f32[128,128]{1,0:T(8,128)}, f32[128,128]{1,0:T(8,128)}, f32[2048,128]{1,0:T(8,128)}, f32[512,128]{0,1:T(8,128)}), (f32[128,128]{1,0:T(8,128)}, f32[128,128]{1,0:T(8,128)}, f32[2048,128]{1,0:T(8,128)}, ...) | async-done | bytes 1441808 | tf_op jit(solution)/shard_map/psum | solution.py:75
  143.0 39.1 %all-gather.2.cloned.1.call-done = f32[2048,128]{1,0:T(8,128)} async-done(((f32[256,128]{1,0:T(8,128)}), f32[2048,128]{1,0:T(8,128)}) %all-gather.2.cloned.1.call-update) | async-done | bytes 1048592 | tf_op jit(solution)/shard_map/all_gather | solution.py:81
  182.8 5.5 collective-permute-start.5
  189.7 15.4 %fusion.13 = f32[512,128]{1,0:T(8,128)S(1)} fusion(f32[]{:T(128)} %bitcast.17, s32[512]{0:T(512)S(1)} %get-tuple-element.63, f32[]{:T(128)} %bitcast.15, s32[512]{0:T(512)S(1)} %get-tuple-element.64, f32[]{:T(128)} %bitcast.13, s32[512]{0:T(512)S(1)} %get-tuple-element.65, f32[]{:T(128)} %bitcast.11, s32[512]{0:T(512)S(1)} %get-tuple-element.66, ...), kind=kOutput, calls=%fused_computation.32 | convolution fusion | flops 1651200000 | bytes 1337380 | tf_op jit(solution)/shard_map/dot_general | solution.py:51
  205.1 5.4 collective-permute-start.7
  210.9 5.7 collective-permute-start.3
  216.6 14.6 %fusion.19 = f32[2048,128]{1,0:T(8,128)S(1)} fusion(f32[]{:T(128)} %bitcast.17, f32[]{:T(128)} %bitcast.15, f32[]{:T(128)} %bitcast.13, f32[]{:T(128)} %bitcast.11, f32[]{:T(128)} %bitcast.9, f32[]{:T(128)} %bitcast.7, f32[]{:T(128)} %bitcast.5, f32[]{:T(128)} %bitcast.3, f32[]{:T(128)} %bitcast.1, s32[516]{0:T(1024)S(1)} %iota_multiply_fusion, ...), kind=kOutput, calls=%fused_computation.40 | convolution fusion | flops 1650803712 | bytes 1388596 | tf_op jit(solution)/shard_map/dot_general | solution.py:51
  233.4 15.0 %fusion.3 = f32[2048,128]{1,0:T(8,128)S(1)} fusion(f32[2048,128]{1,0:T(8,128)S(1)} %fusion.5, f32[2048,128]{1,0:T(8,128)S(1)} %copy-done.8, f32[]{:T(128)} %bitcast.17, f32[]{:T(128)} %bitcast.15, f32[]{:T(128)} %bitcast.13, f32[]{:T(128)} %bitcast.11, f32[]{:T(128)} %bitcast.9, f32[]{:T(128)} %bitcast.7, f32[]{:T(128)} %bitcast.5, f32[]{:T(128)} %bitcast.3, ...), kind=kOutput, calls=%fused_computation.18 | convolution fusion | flops 1651328000 | bytes 3485748 | tf_op jit(solution)/shard_map/dot_general | solution.py:51
  248.4 5.5 collective-permute-start.9
  255.3 14.2 %fusion.12 = f32[512,128]{1,0:T(8,128)S(1)} fusion(f32[]{:T(128)} %bitcast.17, s32[512]{0:T(512)S(1)} %get-tuple-element.63, f32[]{:T(128)} %bitcast.15, s32[512]{0:T(512)S(1)} %get-tuple-element.64, f32[]{:T(128)} %bitcast.13, s32[512]{0:T(512)S(1)} %get-tuple-element.65, f32[]{:T(128)} %bitcast.11, s32[512]{0:T(512)S(1)} %get-tuple-element.66, ...), kind=kOutput, calls=%fused_computation.31 | convolution fusion | flops 1651200000 | bytes 1337380 | tf_op jit(solution)/shard_map/dot_general | solution.py:51
  269.6 5.8 collective-permute-start.11
  276.7 14.7 %fusion.18 = f32[2048,128]{1,0:T(8,128)S(1)} fusion(f32[]{:T(128)} %bitcast.17, f32[]{:T(128)} %bitcast.15, f32[]{:T(128)} %bitcast.13, f32[]{:T(128)} %bitcast.11, f32[]{:T(128)} %bitcast.9, f32[]{:T(128)} %bitcast.7, f32[]{:T(128)} %bitcast.5, f32[]{:T(128)} %bitcast.3, f32[]{:T(128)} %bitcast.1, s32[516]{0:T(1024)S(1)} %iota_multiply_fusion, ...), kind=kOutput, calls=%fused_computation.39 | convolution fusion | flops 1650803712 | bytes 1388596 | tf_op jit(solution)/shard_map/dot_general | solution.py:51
  294.1 39.1 %all-reduce = (f32[]{:T(128)}, f32[]{:T(128)}) all-reduce(f32[]{:T(128)} %get-tuple-element.3, f32[]{:T(128)} %get-tuple-element.2), channel_id=1, replica_groups=mesh['row'=16,'col'=8] {'row'}, use_global_device_ids=true, to_apply=%region_5.6 | all-reduce | flops 2 | bytes 16 | tf_op jit(solution)/shard_map/psum | solution.py:90
  335.4 33.9 %psum.90 = f32[]{:T(128)} all-reduce(f32[]{:T(128)} %multiply_reduce_fusion.5), channel_id=1, replica_groups=mesh['row'=16,'col'=8] {'row'}, use_global_device_ids=true, to_apply=%region_9.10 | all-reduce | flops 1 | bytes 8 | tf_op jit(solution)/shard_map/psum | solution.py:90
  371.0 5.3 collective-permute-start.13
  377.7 14.1 %fusion.11 = f32[512,128]{1,0:T(8,128)S(1)} fusion(f32[]{:T(128)} %bitcast.17, s32[512]{0:T(512)S(1)} %get-tuple-element.63, f32[]{:T(128)} %bitcast.15, s32[512]{0:T(512)S(1)} %get-tuple-element.64, f32[]{:T(128)} %bitcast.13, s32[512]{0:T(512)S(1)} %get-tuple-element.65, f32[]{:T(128)} %bitcast.11, s32[512]{0:T(512)S(1)} %get-tuple-element.66, ...), kind=kOutput, calls=%fused_computation.30 | convolution fusion | flops 1651200000 | bytes 1337380 | tf_op jit(solution)/shard_map/dot_general | solution.py:51
  391.9 5.6 collective-permute-start.15
  398.8 14.5 %fusion.17 = f32[2048,128]{1,0:T(8,128)S(1)} fusion(f32[]{:T(128)} %bitcast.17, f32[]{:T(128)} %bitcast.15, f32[]{:T(128)} %bitcast.13, f32[]{:T(128)} %bitcast.11, f32[]{:T(128)} %bitcast.9, f32[]{:T(128)} %bitcast.7, f32[]{:T(128)} %bitcast.5, f32[]{:T(128)} %bitcast.3, f32[]{:T(128)} %bitcast.1, s32[516]{0:T(1024)S(1)} %iota_multiply_fusion, ...), kind=kOutput, calls=%fused_computation.38 | convolution fusion | flops 1650803712 | bytes 1388596 | tf_op jit(solution)/shard_map/dot_general | solution.py:51
  416.9 39.1 %psum.91 = f32[]{:T(128)} all-reduce(f32[]{:T(128)} %get-tuple-element.57), channel_id=1, replica_groups=mesh['row'=16,'col'=8] {'row'}, use_global_device_ids=true, to_apply=%region_11.12 | all-reduce | flops 1 | bytes 8 | tf_op jit(solution)/shard_map/psum | solution.py:90
  460.4 34.2 %psum.92 = f32[]{:T(128)} all-reduce(f32[]{:T(128)} %get-tuple-element.12), channel_id=1, replica_groups=mesh['row'=16,'col'=8] {'row'}, use_global_device_ids=true, to_apply=%region_13.14 | all-reduce | flops 1 | bytes 8 | tf_op jit(solution)/shard_map/psum | solution.py:90
  504.1 14.1 %fusion.10 = f32[512,128]{1,0:T(8,128)S(1)} fusion(f32[]{:T(128)} %bitcast.17, s32[512]{0:T(512)S(1)} %get-tuple-element.63, f32[]{:T(128)} %bitcast.15, s32[512]{0:T(512)S(1)} %get-tuple-element.64, f32[]{:T(128)} %bitcast.13, s32[512]{0:T(512)S(1)} %get-tuple-element.65, f32[]{:T(128)} %bitcast.11, s32[512]{0:T(512)S(1)} %get-tuple-element.66, ...), kind=kOutput, calls=%fused_computation.29 | convolution fusion | flops 1651200000 | bytes 1337380 | tf_op jit(solution)/shard_map/dot_general | solution.py:51
  518.3 5.6 collective-permute-start.19
  525.2 14.5 %fusion.16 = f32[2048,128]{1,0:T(8,128)S(1)} fusion(f32[]{:T(128)} %bitcast.17, f32[]{:T(128)} %bitcast.15, f32[]{:T(128)} %bitcast.13, f32[]{:T(128)} %bitcast.11, f32[]{:T(128)} %bitcast.9, f32[]{:T(128)} %bitcast.7, f32[]{:T(128)} %bitcast.5, f32[]{:T(128)} %bitcast.3, f32[]{:T(128)} %bitcast.1, s32[516]{0:T(1024)S(1)} %iota_multiply_fusion, ...), kind=kOutput, calls=%fused_computation.37 | convolution fusion | flops 1650803712 | bytes 1388596 | tf_op jit(solution)/shard_map/dot_general | solution.py:51
  543.3 39.1 %psum.93 = f32[]{:T(128)} all-reduce(f32[]{:T(128)} %get-tuple-element.59), channel_id=1, replica_groups=mesh['row'=16,'col'=8] {'row'}, use_global_device_ids=true, to_apply=%region_15.16 | all-reduce | flops 1 | bytes 8 | tf_op jit(solution)/shard_map/psum | solution.py:90
  587.0 33.8 %psum.94 = f32[]{:T(128)} all-reduce(f32[]{:T(128)} %get-tuple-element.10), channel_id=1, replica_groups=mesh['row'=16,'col'=8] {'row'}, use_global_device_ids=true, to_apply=%region_17.18 | all-reduce | flops 1 | bytes 8 | tf_op jit(solution)/shard_map/psum | solution.py:90
  630.5 14.1 %fusion.9 = f32[512,128]{1,0:T(8,128)S(1)} fusion(f32[]{:T(128)} %bitcast.17, s32[512]{0:T(512)S(1)} %get-tuple-element.63, f32[]{:T(128)} %bitcast.15, s32[512]{0:T(512)S(1)} %get-tuple-element.64, f32[]{:T(128)} %bitcast.13, s32[512]{0:T(512)S(1)} %get-tuple-element.65, f32[]{:T(128)} %bitcast.11, s32[512]{0:T(512)S(1)} %get-tuple-element.66, ...), kind=kOutput, calls=%fused_computation.28 | convolution fusion | flops 1651200000 | bytes 1337380 | tf_op jit(solution)/shard_map/dot_general | solution.py:51
  644.7 5.6 collective-permute-start.23
  651.7 15.5 %fusion.15 = f32[2048,128]{1,0:T(8,128)S(1)} fusion(f32[]{:T(128)} %bitcast.17, f32[]{:T(128)} %bitcast.15, f32[]{:T(128)} %bitcast.13, f32[]{:T(128)} %bitcast.11, f32[]{:T(128)} %bitcast.9, f32[]{:T(128)} %bitcast.7, f32[]{:T(128)} %bitcast.5, f32[]{:T(128)} %bitcast.3, f32[]{:T(128)} %bitcast.1, s32[516]{0:T(1024)S(1)} %iota_multiply_fusion, ...), kind=kOutput, calls=%fused_computation.36 | convolution fusion | flops 1650803712 | bytes 1388596 | tf_op jit(solution)/shard_map/dot_general | solution.py:51
  670.7 39.1 %psum.95 = f32[]{:T(128)} all-reduce(f32[]{:T(128)} %get-tuple-element.61), channel_id=1, replica_groups=mesh['row'=16,'col'=8] {'row'}, use_global_device_ids=true, to_apply=%region_19.20 | all-reduce | flops 1 | bytes 8 | tf_op jit(solution)/shard_map/psum | solution.py:90
  (117 shorter events, 86.9 us)
Async XLA Ops:
  7.2 39.3 %copy-start = (f32[2,96]{1,0:T(2,128)S(1)}, f32[2,96]{1,0:T(2,128)}, u32[]{:S(2)}) copy-start(f32[2,96]{1,0:T(2,128)} %param.13) | copy-start | bytes 2308
  7.2 134.7 %all-reduce.4.cloned.1.call-start = ((), (), s32[]{:S(2)}) async-start(), calls=%async_computation.1 | async-start | bytes 2883584 | tf_op jit(solution)/shard_map/psum | solution.py:75
  33.2 19.3 %collective-permute-start = (bf16[8,128]{0,1:T(8,128)(2,1)S(1)}, bf16[8,128]{0,1:T(8,128)(2,1)S(1)}, u32[]{:S(2)}, u32[]{:S(2)}) collective-permute-start(bf16[8,128]{0,1:T(8,128)(2,1)S(1)} %get-tuple-element.36), channel_id=1, source_target_pairs={{0,1},{1,2},{2,3},{3,4},{4,5},{5,6},{6,7},{7,0},{8,9},{9,10},{10,1... | collective-permute-start | bytes 6152 | tf_op jit(solution)/shard_map/ppermute | solution.py:20
  34.7 17.8 %collective-permute-start.1 = (bf16[8,128]{0,1:T(8,128)(2,1)S(1)}, bf16[8,128]{0,1:T(8,128)(2,1)S(1)}, u32[]{:S(2)}, u32[]{:S(2)}) collective-permute-start(bf16[8,128]{0,1:T(8,128)(2,1)S(1)} %get-tuple-element.37), channel_id=1, source_target_pairs={{1,0},{2,1},{3,2},{4,3},{5,4},{6,5},{7,6},{0,7},{9,8},{10,9},{11,1... | collective-permute-start | bytes 6152 | tf_op jit(solution)/shard_map/ppermute | solution.py:22
  47.4 12.4 %copy-start.4 = (f32[96,128]{1,0:T(8,128)S(1)}, f32[96,128]{1,0:T(8,128)}, u32[]{:S(2)}) copy-start(f32[96,128]{1,0:T(8,128)} %param.12) | copy-start | bytes 147460
  68.1 114.0 %all-gather.2.cloned.1.call-start = ((), (), s32[]{:S(2)}) async-start(), calls=%async_computation | async-start | bytes 1179648 | tf_op jit(solution)/shard_map/all_gather | solution.py:81
  182.8 6.6 collective-permute-start.4
  182.8 6.9 collective-permute-start.5
  189.7 20.8 %copy-start.6 = (f32[128,128]{1,0:T(8,128)S(1)}, f32[128,128]{1,0:T(8,128)}, u32[]{:S(2)}) copy-start(f32[128,128]{1,0:T(8,128)} %get-tuple-element.7) | copy-start | bytes 196612
  205.0 11.6 %collective-permute-start.6 = (f32[2,128]{1,0:T(2,128)S(1)}, f32[2,128]{1,0:T(2,128)S(1)}, u32[]{:S(2)}, u32[]{:S(2)}) collective-permute-start(f32[2,128]{1,0:T(2,128)S(1)} %get-tuple-element.34), channel_id=1, source_target_pairs={{0,8},{8,16},{16,24},{24,32},{32,40},{40,48},{48,56},{56,64},{64,7... | collective-permute-start | bytes 3080 | tf_op jit(solution)/shard_map/ppermute | solution.py:20
  205.1 11.5 %collective-permute-start.7 = (f32[2,128]{1,0:T(2,128)S(1)}, f32[2,128]{1,0:T(2,128)S(1)}, u32[]{:S(2)}, u32[]{:S(2)}) collective-permute-start(f32[2,128]{1,0:T(2,128)S(1)} %get-tuple-element.35), channel_id=1, source_target_pairs={{8,0},{16,8},{24,16},{32,24},{40,32},{48,40},{56,48},{64,56},{72,6... | collective-permute-start | bytes 3080 | tf_op jit(solution)/shard_map/ppermute | solution.py:22
  210.8 22.5 %collective-permute-start.2 = (f32[2,128]{0,1:T(8,128)S(1)}, f32[2,128]{0,1:T(8,128)S(1)}, u32[]{:S(2)}, u32[]{:S(2)}) collective-permute-start(f32[2,128]{0,1:T(8,128)S(1)} %get-tuple-element.32), channel_id=1, source_target_pairs={{0,8},{8,16},{16,24},{24,32},{32,40},{40,48},{48,56},{56,64},{64,7... | collective-permute-start | bytes 3080 | tf_op jit(solution)/shard_map/ppermute | solution.py:20
  210.9 22.5 %collective-permute-start.3 = (f32[2,128]{0,1:T(8,128)S(1)}, f32[2,128]{0,1:T(8,128)S(1)}, u32[]{:S(2)}, u32[]{:S(2)}) collective-permute-start(f32[2,128]{0,1:T(8,128)S(1)} %get-tuple-element.33), channel_id=1, source_target_pairs={{8,0},{16,8},{24,16},{32,24},{40,32},{48,40},{56,48},{64,56},{72,6... | collective-permute-start | bytes 3080 | tf_op jit(solution)/shard_map/ppermute | solution.py:22
  216.6 15.6 %copy-start.3 = (f32[2048,128]{1,0:T(8,128)S(1)}, f32[2048,128]{1,0:T(8,128)}, u32[]{:S(2)}) copy-start(f32[2048,128]{1,0:T(8,128)} %all-gather.2.cloned.1.call-done) | copy-start | bytes 3145732
  248.4 6.7 collective-permute-start.8
  248.4 6.9 collective-permute-start.9
  269.5 6.7 collective-permute-start.10
  269.6 7.1 collective-permute-start.11
  370.9 6.7 collective-permute-start.12
  371.0 6.7 collective-permute-start.13
  391.8 6.7 collective-permute-start.14
  391.9 6.9 collective-permute-start.15
  497.3 6.7 collective-permute-start.16
  497.4 6.7 collective-permute-start.17
  518.2 6.7 collective-permute-start.18
  518.3 6.9 collective-permute-start.19
  623.5 21.1 %copy-start.1 = (f32[2048,128]{1,0:T(8,128)}, f32[2048,128]{1,0:T(8,128)S(1)}, u32[]{:S(2)}) copy-start(f32[2048,128]{1,0:T(8,128)S(1)} %multiply_add_fusion) | copy-start | bytes 3145732
  623.5 6.9 collective-permute-start.20
  623.8 6.7 collective-permute-start.21
  644.7 6.7 collective-permute-start.22
  644.7 6.9 collective-permute-start.23
  650.4 17.8 %copy-start.2 = (f32[2048,128]{1,0:T(8,128)S(1)}, f32[2048,128]{1,0:T(8,128)}, u32[]{:S(2)}) copy-start(f32[2048,128]{1,0:T(8,128)} %copy-done.1) | copy-start | bytes 3145732
  (3 other events, 10.0 us)
Sparse Core Ops, SparseCore 0:
  68.2 73.6 all-reduce.3
  143.5 38.5 all-gather.1
where the time goes:
time: 728 us; the launch traced here: 722 us
  blocking collectives  284 us (39%)
  matrix products  199 us (27%)
  waiting for transfers between devices  113 us (16%)
  starting transfers between devices  66 us (9%)
  other arithmetic  30.2 us (4%)
  between operations  24.4 us (3%)
    psum x7, blocking collectives, inner_sum(): return lax.psum(jnp.sum(first_field * second_field), 'row')  258 us
    dot_general x12, matrix products, apply_band(): return jnp.dot(matrix, values.astype(jnp.float32), precision=FULL_PRECISION)  167 us
    ppermute x12, starting transfers between devices, extended(): lax.ppermute(head, axis, [((i + 1) % count, i) for i in range(count)])  63.5 us
    psum x1, waiting for transfers between devices, body(): column_gram, coarse_gram = lax.psum((column_part, coarse_part), 'col')  62 us
    all_gather x1, waiting for transfers between devices, body(): start_rows = lax.all_gather(row_start, 'col', axis=0, tiled=True)  39.1 us
    all_gather x1, blocking collectives, body(): columns = lax.all_gather(col_factor, 'row', axis=1, tiled=True)  25.9 us
  transfers between devices with their start and end apart: 26, of which 17 were waited for; matrix products, arithmetic and copies ran while one was open for 6% of the time, Pallas kernels for 0%

commit v1 on v0

--- a/solution.py
+++ b/solution.py
@@ -78,7 +78,9 @@
     hyper_gram = coarse_gram * band_gram
     multi_gram = column_gram * merged_gram
     multi_sums, hyper_sums = lax.psum((multi_part, hyper_part), "col")
-    start_rows = lax.all_gather(row_start, "col", axis=0, tiled=True)
+    start_rows = jnp.concatenate(
+        lax.all_to_all(jnp.stack([row_start] * lax.axis_size("col")), "col", 0, 0), axis=0
+    )
 
     def fine_rim(values, breadth):
         return extended(values, (("row", 0),), breadth)

time: 728 us -> 672 us (0.923)
  waiting for transfers between devices: 113 us -> 52.4 us
    all_gather x1 -> x0, waiting for transfers between devices: 39.1 us -> none  [body(): start_rows = lax.all_gather(row_start, 'col', axis=0, tiled=True)]
    psum x1, waiting for transfers between devices: 62 us -> 40.2 us  [body(): column_gram, coarse_gram = lax.psum((column_part, coarse_part), 'col')]
  transfers between devices with their start and end apart: 26 -> 26, of which waited for: 17 -> 18; matrix products, arithmetic and copies ran while one was open for 6% -> 11% of each run, Pallas kernels for 0% -> 0%
where the time goes in v1:
time: 672 us; the launch traced here: 666 us
  blocking collectives  284 us (42%)
  matrix products  199 us (30%)
  starting transfers between devices  69.8 us (10%)
  waiting for transfers between devices  52.4 us (8%)
  other arithmetic  30.2 us (4%)
  between operations  24.4 us (4%)
    psum x7, blocking collectives, inner_sum(): return lax.psum(jnp.sum(first_field * second_field), 'row')  258 us
    dot_general x12, matrix products, apply_band(): return jnp.dot(matrix, values.astype(jnp.float32), precision=FULL_PRECISION)  166 us
    ppermute x12, starting transfers between devices, extended(): lax.ppermute(head, axis, [((i + 1) % count, i) for i in range(count)])  63.6 us
    psum x1, waiting for transfers between devices, body(): column_gram, coarse_gram = lax.psum((column_part, coarse_part), 'col')  40.2 us
    all_gather x1, blocking collectives, body(): columns = lax.all_gather(col_factor, 'row', axis=1, tiled=True)  25.9 us
  transfers between devices with their start and end apart: 26, of which 18 were waited for; matrix products, arithmetic and copies ran while one was open for 11% of the time, Pallas kernels for 0%

profile of v1, /device:TPU:0, one launch (start us, length us, event | category | flops | bytes accessed | tf_op | source)
XLA Modules:
  0.0 666.0 jit_solution(5651289299841598301)
XLA Ops:
  7.2 25.9 %all_gather.3 = bf16[512,128]{0,1:T(8,128)(2,1)S(1)} all-gather(bf16[512,8]{0,1:T(8,128)(2,1)} %param.11), channel_id=1, replica_groups=mesh['row'=16,'col'=8] {'row'}, dimensions={1}, use_global_device_ids=true | all-gather | bytes 139264 | tf_op jit(solution)/shard_map/all_gather | solution.py:58
  68.4 6.4 fusion.50
  74.9 8.2 %fusion.14 = f32[512,128]{0,1:T(8,128)} fusion(bf16[96,512,128]{2,1,0:T(8,128)(2,1)} %param.9, f32[128,128]{0,1:T(8,128)S(1)} %copy.10, f32[96,128]{1,0:T(8,128)S(1)} %copy-done.4), kind=kOutput, calls=%fused_computation.33 | convolution fusion | flops 1613758464 | bytes 12959744 | tf_op jit(solution)/shard_map/kij,kjr->ir/dot_general | solution.py:70
  83.1 5.5 collective-permute-start.5
  90.0 14.2 %fusion.13 = f32[512,128]{1,0:T(8,128)S(1)} fusion(f32[]{:T(128)} %bitcast.18, s32[512]{0:T(512)S(1)} %get-tuple-element.63, f32[]{:T(128)} %bitcast.16, s32[512]{0:T(512)S(1)} %get-tuple-element.64, f32[]{:T(128)} %bitcast.14, s32[512]{0:T(512)S(1)} %get-tuple-element.65, f32[]{:T(128)} %bitcast.12, s32[512]{0:T(512)S(1)} %get-tuple-element.66, ...), kind=kOutput, calls=%fused_computation.32 | convolution fusion | flops 1651200000 | bytes 1337380 | tf_op jit(solution)/shard_map/dot_general | solution.py:51
  104.3 5.8 collective-permute-start.7
  111.4 14.8 %fusion.19 = f32[2048,128]{1,0:T(8,128)S(1)} fusion(f32[]{:T(128)} %bitcast.18, f32[]{:T(128)} %bitcast.16, f32[]{:T(128)} %bitcast.14, f32[]{:T(128)} %bitcast.12, f32[]{:T(128)} %bitcast.10, f32[]{:T(128)} %bitcast.8, f32[]{:T(128)} %bitcast.6, f32[]{:T(128)} %bitcast.4, f32[]{:T(128)} %bitcast.2, s32[516]{0:T(1024)S(1)} %iota_multiply_fusion, ...), kind=kOutput, calls=%fused_computation.40 | convolution fusion | flops 1650803712 | bytes 1388596 | tf_op jit(solution)/shard_map/dot_general | solution.py:51
  126.2 40.2 %all-reduce.4.cloned.1.call-done = (f32[128,128]{1,0:T(8,128)}, f32[128,128]{1,0:T(8,128)}, f32[2048,128]{1,0:T(8,128)}, f32[512,128]{0,1:T(8,128)}) async-done(((f32[128,128]{1,0:T(8,128)}, f32[128,128]{1,0:T(8,128)}, f32[2048,128]{1,0:T(8,128)}, f32[512,128]{0,1:T(8,128)}), (f32[128,128]{1,0:T(8,128)}, f32[128,128]{1,0:T(8,128)}, f32[2048,128]{1,0:T(8,128)}, ...) | async-done | bytes 1441808 | tf_op jit(solution)/shard_map/psum | solution.py:75
  169.8 5.5 collective-permute-start.3
  177.4 14.9 %fusion.3 = f32[2048,128]{1,0:T(8,128)S(1)} fusion(f32[2048,128]{1,0:T(8,128)S(1)} %fusion.5, f32[2048,128]{1,0:T(8,128)S(1)} %copy-done.7, f32[]{:T(128)} %bitcast.18, f32[]{:T(128)} %bitcast.16, f32[]{:T(128)} %bitcast.14, f32[]{:T(128)} %bitcast.12, f32[]{:T(128)} %bitcast.10, f32[]{:T(128)} %bitcast.8, f32[]{:T(128)} %bitcast.6, f32[]{:T(128)} %bitcast.4, ...), kind=kOutput, calls=%fused_computation.18 | convolution fusion | flops 1651328000 | bytes 3485748 | tf_op jit(solution)/shard_map/dot_general | solution.py:51
  192.4 5.5 collective-permute-start.9
  199.3 14.2 %fusion.12 = f32[512,128]{1,0:T(8,128)S(1)} fusion(f32[]{:T(128)} %bitcast.18, s32[512]{0:T(512)S(1)} %get-tuple-element.63, f32[]{:T(128)} %bitcast.16, s32[512]{0:T(512)S(1)} %get-tuple-element.64, f32[]{:T(128)} %bitcast.14, s32[512]{0:T(512)S(1)} %get-tuple-element.65, f32[]{:T(128)} %bitcast.12, s32[512]{0:T(512)S(1)} %get-tuple-element.66, ...), kind=kOutput, calls=%fused_computation.31 | convolution fusion | flops 1651200000 | bytes 1337380 | tf_op jit(solution)/shard_map/dot_general | solution.py:51
  213.6 5.8 collective-permute-start.11
  220.7 14.6 %fusion.18 = f32[2048,128]{1,0:T(8,128)S(1)} fusion(f32[]{:T(128)} %bitcast.18, f32[]{:T(128)} %bitcast.16, f32[]{:T(128)} %bitcast.14, f32[]{:T(128)} %bitcast.12, f32[]{:T(128)} %bitcast.10, f32[]{:T(128)} %bitcast.8, f32[]{:T(128)} %bitcast.6, f32[]{:T(128)} %bitcast.4, f32[]{:T(128)} %bitcast.2, s32[516]{0:T(1024)S(1)} %iota_multiply_fusion, ...), kind=kOutput, calls=%fused_computation.39 | convolution fusion | flops 1650803712 | bytes 1388596 | tf_op jit(solution)/shard_map/dot_general | solution.py:51
  238.0 39.1 %all-reduce = (f32[]{:T(128)}, f32[]{:T(128)}) all-reduce(f32[]{:T(128)} %get-tuple-element.3, f32[]{:T(128)} %get-tuple-element.2), channel_id=1, replica_groups=mesh['row'=16,'col'=8] {'row'}, use_global_device_ids=true, to_apply=%region_5.6 | all-reduce | flops 2 | bytes 16 | tf_op jit(solution)/shard_map/psum | solution.py:92
  279.3 33.9 %psum.90 = f32[]{:T(128)} all-reduce(f32[]{:T(128)} %multiply_reduce_fusion.5), channel_id=1, replica_groups=mesh['row'=16,'col'=8] {'row'}, use_global_device_ids=true, to_apply=%region_9.10 | all-reduce | flops 1 | bytes 8 | tf_op jit(solution)/shard_map/psum | solution.py:92
  314.8 5.3 collective-permute-start.13
  321.5 14.2 %fusion.11 = f32[512,128]{1,0:T(8,128)S(1)} fusion(f32[]{:T(128)} %bitcast.18, s32[512]{0:T(512)S(1)} %get-tuple-element.63, f32[]{:T(128)} %bitcast.16, s32[512]{0:T(512)S(1)} %get-tuple-element.64, f32[]{:T(128)} %bitcast.14, s32[512]{0:T(512)S(1)} %get-tuple-element.65, f32[]{:T(128)} %bitcast.12, s32[512]{0:T(512)S(1)} %get-tuple-element.66, ...), kind=kOutput, calls=%fused_computation.30 | convolution fusion | flops 1651200000 | bytes 1337380 | tf_op jit(solution)/shard_map/dot_general | solution.py:51
  335.8 5.6 collective-permute-start.15
  342.7 14.6 %fusion.17 = f32[2048,128]{1,0:T(8,128)S(1)} fusion(f32[]{:T(128)} %bitcast.18, f32[]{:T(128)} %bitcast.16, f32[]{:T(128)} %bitcast.14, f32[]{:T(128)} %bitcast.12, f32[]{:T(128)} %bitcast.10, f32[]{:T(128)} %bitcast.8, f32[]{:T(128)} %bitcast.6, f32[]{:T(128)} %bitcast.4, f32[]{:T(128)} %bitcast.2, s32[516]{0:T(1024)S(1)} %iota_multiply_fusion, ...), kind=kOutput, calls=%fused_computation.38 | convolution fusion | flops 1650803712 | bytes 1388596 | tf_op jit(solution)/shard_map/dot_general | solution.py:51
  360.9 39.1 %psum.91 = f32[]{:T(128)} all-reduce(f32[]{:T(128)} %get-tuple-element.57), channel_id=1, replica_groups=mesh['row'=16,'col'=8] {'row'}, use_global_device_ids=true, to_apply=%region_11.12 | all-reduce | flops 1 | bytes 8 | tf_op jit(solution)/shard_map/psum | solution.py:92
  404.4 34.2 %psum.92 = f32[]{:T(128)} all-reduce(f32[]{:T(128)} %get-tuple-element.12), channel_id=1, replica_groups=mesh['row'=16,'col'=8] {'row'}, use_global_device_ids=true, to_apply=%region_13.14 | all-reduce | flops 1 | bytes 8 | tf_op jit(solution)/shard_map/psum | solution.py:92
  441.4 5.3 collective-permute-start.17
  448.1 14.2 %fusion.10 = f32[512,128]{1,0:T(8,128)S(1)} fusion(f32[]{:T(128)} %bitcast.18, s32[512]{0:T(512)S(1)} %get-tuple-element.63, f32[]{:T(128)} %bitcast.16, s32[512]{0:T(512)S(1)} %get-tuple-element.64, f32[]{:T(128)} %bitcast.14, s32[512]{0:T(512)S(1)} %get-tuple-element.65, f32[]{:T(128)} %bitcast.12, s32[512]{0:T(512)S(1)} %get-tuple-element.66, ...), kind=kOutput, calls=%fused_computation.29 | convolution fusion | flops 1651200000 | bytes 1337380 | tf_op jit(solution)/shard_map/dot_general | solution.py:51
  462.4 5.6 collective-permute-start.19
  469.2 14.6 %fusion.16 = f32[2048,128]{1,0:T(8,128)S(1)} fusion(f32[]{:T(128)} %bitcast.18, f32[]{:T(128)} %bitcast.16, f32[]{:T(128)} %bitcast.14, f32[]{:T(128)} %bitcast.12, f32[]{:T(128)} %bitcast.10, f32[]{:T(128)} %bitcast.8, f32[]{:T(128)} %bitcast.6, f32[]{:T(128)} %bitcast.4, f32[]{:T(128)} %bitcast.2, s32[516]{0:T(1024)S(1)} %iota_multiply_fusion, ...), kind=kOutput, calls=%fused_computation.37 | convolution fusion | flops 1650803712 | bytes 1388596 | tf_op jit(solution)/shard_map/dot_general | solution.py:51
  487.4 39.1 %psum.93 = f32[]{:T(128)} all-reduce(f32[]{:T(128)} %get-tuple-element.59), channel_id=1, replica_groups=mesh['row'=16,'col'=8] {'row'}, use_global_device_ids=true, to_apply=%region_15.16 | all-reduce | flops 1 | bytes 8 | tf_op jit(solution)/shard_map/psum | solution.py:92
  531.2 33.8 %psum.94 = f32[]{:T(128)} all-reduce(f32[]{:T(128)} %get-tuple-element.10), channel_id=1, replica_groups=mesh['row'=16,'col'=8] {'row'}, use_global_device_ids=true, to_apply=%region_17.18 | all-reduce | flops 1 | bytes 8 | tf_op jit(solution)/shard_map/psum | solution.py:92
  574.7 14.2 %fusion.9 = f32[512,128]{1,0:T(8,128)S(1)} fusion(f32[]{:T(128)} %bitcast.18, s32[512]{0:T(512)S(1)} %get-tuple-element.63, f32[]{:T(128)} %bitcast.16, s32[512]{0:T(512)S(1)} %get-tuple-element.64, f32[]{:T(128)} %bitcast.14, s32[512]{0:T(512)S(1)} %get-tuple-element.65, f32[]{:T(128)} %bitcast.12, s32[512]{0:T(512)S(1)} %get-tuple-element.66, ...), kind=kOutput, calls=%fused_computation.28 | convolution fusion | flops 1651200000 | bytes 1337380 | tf_op jit(solution)/shard_map/dot_general | solution.py:51
  589.0 5.6 collective-permute-start.23
  595.9 15.5 %fusion.15 = f32[2048,128]{1,0:T(8,128)S(1)} fusion(f32[]{:T(128)} %bitcast.18, f32[]{:T(128)} %bitcast.16, f32[]{:T(128)} %bitcast.14, f32[]{:T(128)} %bitcast.12, f32[]{:T(128)} %bitcast.10, f32[]{:T(128)} %bitcast.8, f32[]{:T(128)} %bitcast.6, f32[]{:T(128)} %bitcast.4, f32[]{:T(128)} %bitcast.2, s32[516]{0:T(1024)S(1)} %iota_multiply_fusion, ...), kind=kOutput, calls=%fused_computation.36 | convolution fusion | flops 1650803712 | bytes 1388596 | tf_op jit(solution)/shard_map/dot_general | solution.py:51
  615.0 39.1 %psum.95 = f32[]{:T(128)} all-reduce(f32[]{:T(128)} %get-tuple-element.61), channel_id=1, replica_groups=mesh['row'=16,'col'=8] {'row'}, use_global_device_ids=true, to_apply=%region_19.20 | all-reduce | flops 1 | bytes 8 | tf_op jit(solution)/shard_map/psum | solution.py:92
  (115 shorter events, 87.3 us)
Async XLA Ops:
  7.2 55.9 %copy-start = (f32[2,96]{1,0:T(2,128)S(1)}, f32[2,96]{1,0:T(2,128)}, u32[]{:S(2)}) copy-start(f32[2,96]{1,0:T(2,128)} %param.13) | copy-start | bytes 2308
  7.2 55.9 %copy-start.4 = (f32[96,128]{1,0:T(8,128)S(1)}, f32[96,128]{1,0:T(8,128)}, u32[]{:S(2)}) copy-start(f32[96,128]{1,0:T(8,128)} %param.12) | copy-start | bytes 147460
  33.2 35.2 %collective-permute-start = (bf16[8,128]{0,1:T(8,128)(2,1)S(1)}, bf16[8,128]{0,1:T(8,128)(2,1)S(1)}, u32[]{:S(2)}, u32[]{:S(2)}) collective-permute-start(bf16[8,128]{0,1:T(8,128)(2,1)S(1)} %get-tuple-element.36), channel_id=1, source_target_pairs={{0,1},{1,2},{2,3},{3,4},{4,5},{5,6},{6,7},{7,0},{8,9},{9,10},{10,1... | collective-permute-start | bytes 6152 | tf_op jit(solution)/shard_map/ppermute | solution.py:20
  34.7 33.7 %collective-permute-start.1 = (bf16[8,128]{0,1:T(8,128)(2,1)S(1)}, bf16[8,128]{0,1:T(8,128)(2,1)S(1)}, u32[]{:S(2)}, u32[]{:S(2)}) collective-permute-start(bf16[8,128]{0,1:T(8,128)(2,1)S(1)} %get-tuple-element.37), channel_id=1, source_target_pairs={{1,0},{2,1},{3,2},{4,3},{5,4},{6,5},{7,6},{0,7},{9,8},{10,9},{11,1... | collective-permute-start | bytes 6152 | tf_op jit(solution)/shard_map/ppermute | solution.py:22
  39.3 43.7 %all-to-all-start = ((f32[8,256,128]{2,1,0:T(8,128)}), f32[8,256,128]{2,1,0:T(8,128)S(1)}, u32[]{:S(2)}, u32[]{:S(2)}) async-start(f32[8,256,128]{2,1,0:T(8,128)} %stack.2), calls=%async_computation | async-start | bytes 2097152 | tf_op jit(solution)/shard_map/all_to_all | solution.py:82
  42.9 123.6 %all-reduce.4.cloned.1.call-start = ((), (), s32[]{:S(2)}) async-start(), calls=%async_computation.1 | async-start | bytes 2883584 | tf_op jit(solution)/shard_map/psum | solution.py:75
  83.0 93.3 %copy-start.1 = (f32[8,256,128]{2,1,0:T(8,128)}, f32[8,256,128]{2,1,0:T(8,128)S(1)}, u32[]{:S(2)}) copy-start(f32[8,256,128]{2,1,0:T(8,128)S(1)} %all-to-all-done) | copy-start | bytes 3145732
  83.0 6.7 %collective-permute-start.4 = (f32[8,128]{1,0:T(8,128)S(1)}, f32[8,128]{1,0:T(8,128)S(1)}, u32[]{:S(2)}, u32[]{:S(2)}) collective-permute-start(f32[8,128]{1,0:T(8,128)S(1)} %get-tuple-element.22), channel_id=1, source_target_pairs={{0,8},{8,16},{16,24},{24,32},{32,40},{40,48},{48,56},{56,64},{64,7... | collective-permute-start | bytes 12296 | tf_op jit(solution)/shard_map/ppermute | solution.py:20
  83.1 6.9 %collective-permute-start.5 = (f32[8,128]{1,0:T(8,128)S(1)}, f32[8,128]{1,0:T(8,128)S(1)}, u32[]{:S(2)}, u32[]{:S(2)}) collective-permute-start(f32[8,128]{1,0:T(8,128)S(1)} %get-tuple-element.23), channel_id=1, source_target_pairs={{8,0},{16,8},{24,16},{32,24},{40,32},{48,40},{56,48},{64,56},{72,6... | collective-permute-start | bytes 12296 | tf_op jit(solution)/shard_map/ppermute | solution.py:22
  104.2 6.7 %collective-permute-start.6 = (f32[2,128]{1,0:T(2,128)S(1)}, f32[2,128]{1,0:T(2,128)S(1)}, u32[]{:S(2)}, u32[]{:S(2)}) collective-permute-start(f32[2,128]{1,0:T(2,128)S(1)} %get-tuple-element.34), channel_id=1, source_target_pairs={{0,8},{8,16},{16,24},{24,32},{32,40},{40,48},{48,56},{56,64},{64,7... | collective-permute-start | bytes 3080 | tf_op jit(solution)/shard_map/ppermute | solution.py:20
  104.3 7.1 %collective-permute-start.7 = (f32[2,128]{1,0:T(2,128)S(1)}, f32[2,128]{1,0:T(2,128)S(1)}, u32[]{:S(2)}, u32[]{:S(2)}) collective-permute-start(f32[2,128]{1,0:T(2,128)S(1)} %get-tuple-element.35), channel_id=1, source_target_pairs={{8,0},{16,8},{24,16},{32,24},{40,32},{48,40},{56,48},{64,56},{72,6... | collective-permute-start | bytes 3080 | tf_op jit(solution)/shard_map/ppermute | solution.py:22
  166.4 11.0 %copy-start.7 = (f32[2048,128]{1,0:T(8,128)S(1)}, f32[2048,128]{1,0:T(8,128)}, u32[]{:S(2)}) copy-start(f32[2048,128]{1,0:T(8,128)} %get-tuple-element.8) | copy-start | bytes 3145732
  169.8 7.6 %collective-permute-start.2 = (f32[2,128]{0,1:T(8,128)S(1)}, f32[2,128]{0,1:T(8,128)S(1)}, u32[]{:S(2)}, u32[]{:S(2)}) collective-permute-start(f32[2,128]{0,1:T(8,128)S(1)} %get-tuple-element.32), channel_id=1, source_target_pairs={{0,8},{8,16},{16,24},{24,32},{32,40},{40,48},{48,56},{56,64},{64,7... | collective-permute-start | bytes 3080 | tf_op jit(solution)/shard_map/ppermute | solution.py:20
  169.8 7.6 %collective-permute-start.3 = (f32[2,128]{0,1:T(8,128)S(1)}, f32[2,128]{0,1:T(8,128)S(1)}, u32[]{:S(2)}, u32[]{:S(2)}) collective-permute-start(f32[2,128]{0,1:T(8,128)S(1)} %get-tuple-element.33), channel_id=1, source_target_pairs={{8,0},{16,8},{24,16},{32,24},{40,32},{48,40},{56,48},{64,56},{72,6... | collective-permute-start | bytes 3080 | tf_op jit(solution)/shard_map/ppermute | solution.py:22
  192.3 6.7 %collective-permute-start.8 = (f32[8,128]{1,0:T(8,128)S(1)}, f32[8,128]{1,0:T(8,128)S(1)}, u32[]{:S(2)}, u32[]{:S(2)}) collective-permute-start(f32[8,128]{1,0:T(8,128)S(1)} %get-tuple-element.20), channel_id=1, source_target_pairs={{0,8},{8,16},{16,24},{24,32},{32,40},{40,48},{48,56},{56,64},{64,7... | collective-permute-start | bytes 12296 | tf_op jit(solution)/shard_map/ppermute | solution.py:20
  192.4 6.9 %collective-permute-start.9 = (f32[8,128]{1,0:T(8,128)S(1)}, f32[8,128]{1,0:T(8,128)S(1)}, u32[]{:S(2)}, u32[]{:S(2)}) collective-permute-start(f32[8,128]{1,0:T(8,128)S(1)} %get-tuple-element.21), channel_id=1, source_target_pairs={{8,0},{16,8},{24,16},{32,24},{40,32},{48,40},{56,48},{64,56},{72,6... | collective-permute-start | bytes 12296 | tf_op jit(solution)/shard_map/ppermute | solution.py:22
  213.5 6.7 %collective-permute-start.10 = (f32[2,128]{1,0:T(2,128)S(1)}, f32[2,128]{1,0:T(2,128)S(1)}, u32[]{:S(2)}, u32[]{:S(2)}) collective-permute-start(f32[2,128]{1,0:T(2,128)S(1)} %get-tuple-element.30), channel_id=1, source_target_pairs={{0,8},{8,16},{16,24},{24,32},{32,40},{40,48},{48,56},{56,64},{64,7... | collective-permute-start | bytes 3080 | tf_op jit(solution)/shard_map/ppermute | solution.py:20
  213.6 7.1 %collective-permute-start.11 = (f32[2,128]{1,0:T(2,128)S(1)}, f32[2,128]{1,0:T(2,128)S(1)}, u32[]{:S(2)}, u32[]{:S(2)}) collective-permute-start(f32[2,128]{1,0:T(2,128)S(1)} %get-tuple-element.31), channel_id=1, source_target_pairs={{8,0},{16,8},{24,16},{32,24},{40,32},{48,40},{56,48},{64,56},{72,6... | collective-permute-start | bytes 3080 | tf_op jit(solution)/shard_map/ppermute | solution.py:22
  314.8 6.7 %collective-permute-start.12 = (f32[8,128]{1,0:T(8,128)S(1)}, f32[8,128]{1,0:T(8,128)S(1)}, u32[]{:S(2)}, u32[]{:S(2)}) collective-permute-start(f32[8,128]{1,0:T(8,128)S(1)} %get-tuple-element.18), channel_id=1, source_target_pairs={{0,8},{8,16},{16,24},{24,32},{32,40},{40,48},{48,56},{56,64},{64,7... | collective-permute-start | bytes 12296 | tf_op jit(solution)/shard_map/ppermute | solution.py:20
  314.8 6.7 %collective-permute-start.13 = (f32[8,128]{1,0:T(8,128)S(1)}, f32[8,128]{1,0:T(8,128)S(1)}, u32[]{:S(2)}, u32[]{:S(2)}) collective-permute-start(f32[8,128]{1,0:T(8,128)S(1)} %get-tuple-element.19), channel_id=1, source_target_pairs={{8,0},{16,8},{24,16},{32,24},{40,32},{48,40},{56,48},{64,56},{72,6... | collective-permute-start | bytes 12296 | tf_op jit(solution)/shard_map/ppermute | solution.py:22
  335.7 6.7 %collective-permute-start.14 = (f32[2,128]{1,0:T(2,128)S(1)}, f32[2,128]{1,0:T(2,128)S(1)}, u32[]{:S(2)}, u32[]{:S(2)}) collective-permute-start(f32[2,128]{1,0:T(2,128)S(1)} %get-tuple-element.28), channel_id=1, source_target_pairs={{0,8},{8,16},{16,24},{24,32},{32,40},{40,48},{48,56},{56,64},{64,7... | collective-permute-start | bytes 3080 | tf_op jit(solution)/shard_map/ppermute | solution.py:20
  335.8 6.9 %collective-permute-start.15 = (f32[2,128]{1,0:T(2,128)S(1)}, f32[2,128]{1,0:T(2,128)S(1)}, u32[]{:S(2)}, u32[]{:S(2)}) collective-permute-start(f32[2,128]{1,0:T(2,128)S(1)} %get-tuple-element.29), channel_id=1, source_target_pairs={{8,0},{16,8},{24,16},{32,24},{40,32},{48,40},{56,48},{64,56},{72,6... | collective-permute-start | bytes 3080 | tf_op jit(solution)/shard_map/ppermute | solution.py:22
  441.4 6.7 %collective-permute-start.16 = (f32[8,128]{1,0:T(8,128)S(1)}, f32[8,128]{1,0:T(8,128)S(1)}, u32[]{:S(2)}, u32[]{:S(2)}) collective-permute-start(f32[8,128]{1,0:T(8,128)S(1)} %get-tuple-element.16), channel_id=1, source_target_pairs={{0,8},{8,16},{16,24},{24,32},{32,40},{40,48},{48,56},{56,64},{64,7... | collective-permute-start | bytes 12296 | tf_op jit(solution)/shard_map/ppermute | solution.py:20
  441.4 6.7 %collective-permute-start.17 = (f32[8,128]{1,0:T(8,128)S(1)}, f32[8,128]{1,0:T(8,128)S(1)}, u32[]{:S(2)}, u32[]{:S(2)}) collective-permute-start(f32[8,128]{1,0:T(8,128)S(1)} %get-tuple-element.17), channel_id=1, source_target_pairs={{8,0},{16,8},{24,16},{32,24},{40,32},{48,40},{56,48},{64,56},{72,6... | collective-permute-start | bytes 12296 | tf_op jit(solution)/shard_map/ppermute | solution.py:22
  462.3 6.7 %collective-permute-start.18 = (f32[2,128]{1,0:T(2,128)S(1)}, f32[2,128]{1,0:T(2,128)S(1)}, u32[]{:S(2)}, u32[]{:S(2)}) collective-permute-start(f32[2,128]{1,0:T(2,128)S(1)} %get-tuple-element.26), channel_id=1, source_target_pairs={{0,8},{8,16},{16,24},{24,32},{32,40},{40,48},{48,56},{56,64},{64,7... | collective-permute-start | bytes 3080 | tf_op jit(solution)/shard_map/ppermute | solution.py:20
  462.4 6.9 %collective-permute-start.19 = (f32[2,128]{1,0:T(2,128)S(1)}, f32[2,128]{1,0:T(2,128)S(1)}, u32[]{:S(2)}, u32[]{:S(2)}) collective-permute-start(f32[2,128]{1,0:T(2,128)S(1)} %get-tuple-element.27), channel_id=1, source_target_pairs={{8,0},{16,8},{24,16},{32,24},{40,32},{48,40},{56,48},{64,56},{72,6... | collective-permute-start | bytes 3080 | tf_op jit(solution)/shard_map/ppermute | solution.py:22
  567.7 21.2 %copy-start.2 = (f32[2048,128]{1,0:T(8,128)}, f32[2048,128]{1,0:T(8,128)S(1)}, u32[]{:S(2)}) copy-start(f32[2048,128]{1,0:T(8,128)S(1)} %multiply_add_fusion) | copy-start | bytes 3145732
  567.7 6.9 %collective-permute-start.20 = (f32[8,128]{1,0:T(8,128)S(1)}, f32[8,128]{1,0:T(8,128)S(1)}, u32[]{:S(2)}, u32[]{:S(2)}) collective-permute-start(f32[8,128]{1,0:T(8,128)S(1)} %get-tuple-element.14), channel_id=1, source_target_pairs={{0,8},{8,16},{16,24},{24,32},{32,40},{40,48},{48,56},{56,64},{64,7... | collective-permute-start | bytes 12296 | tf_op jit(solution)/shard_map/ppermute | solution.py:20
  568.0 6.7 %collective-permute-start.21 = (f32[8,128]{1,0:T(8,128)S(1)}, f32[8,128]{1,0:T(8,128)S(1)}, u32[]{:S(2)}, u32[]{:S(2)}) collective-permute-start(f32[8,128]{1,0:T(8,128)S(1)} %get-tuple-element.15), channel_id=1, source_target_pairs={{8,0},{16,8},{24,16},{32,24},{40,32},{48,40},{56,48},{64,56},{72,6... | collective-permute-start | bytes 12296 | tf_op jit(solution)/shard_map/ppermute | solution.py:22
  588.9 6.7 %collective-permute-start.22 = (f32[2,128]{1,0:T(2,128)S(1)}, f32[2,128]{1,0:T(2,128)S(1)}, u32[]{:S(2)}, u32[]{:S(2)}) collective-permute-start(f32[2,128]{1,0:T(2,128)S(1)} %get-tuple-element.24), channel_id=1, source_target_pairs={{0,8},{8,16},{16,24},{24,32},{32,40},{40,48},{48,56},{56,64},{64,7... | collective-permute-start | bytes 3080 | tf_op jit(solution)/shard_map/ppermute | solution.py:20
  589.0 6.9 %collective-permute-start.23 = (f32[2,128]{1,0:T(2,128)S(1)}, f32[2,128]{1,0:T(2,128)S(1)}, u32[]{:S(2)}, u32[]{:S(2)}) collective-permute-start(f32[2,128]{1,0:T(2,128)S(1)} %get-tuple-element.25), channel_id=1, source_target_pairs={{8,0},{16,8},{24,16},{32,24},{40,32},{48,40},{56,48},{64,56},{72,6... | collective-permute-start | bytes 3080 | tf_op jit(solution)/shard_map/ppermute | solution.py:22
  594.6 17.8 %copy-start.3 = (f32[2048,128]{1,0:T(8,128)S(1)}, f32[2048,128]{1,0:T(8,128)}, u32[]{:S(2)}) copy-start(f32[2048,128]{1,0:T(8,128)} %copy-done.2) | copy-start | bytes 3145732
  (2 other events, 16.7 us)
Sparse Core Ops, SparseCore 0:
  89.7 76.6 all-reduce.3
